TPU v7x, 32 devices: a whole 2x2x4 slice. The times are simulated.
32 devices in a mesh: groups: 2 (over y), ctx: 16 (over z, x, core).
Axes of the slice: x: 2, y: 2, z: 4, core: 2. Of those that a mesh axis runs over, the one named last changes fastest.
Arguments:
- child_q: bfloat16 [32, 128, 4096], P(('groups', 'ctx')), parts along dimension 0, may hold values from -8 to 8
- child_kv: bfloat16 [32, 128, 2, 512], P(('groups', 'ctx')), parts along dimension 0, may hold values from -12 to 12
- prompt_kv: bfloat16 [128, 2, 512], P(('groups', 'ctx')), parts along dimension 0, may hold values from -12 to 12
- parent_kv: bfloat16 [256, 2, 2, 512], P(('groups', 'ctx')), parts along dimension 0, may hold values from -12 to 12
- fork_list: int32 [32], P('groups'), parts along dimension 0, may hold values from 0 to 1
- owner_map: int32 [4, 16], P('groups'), parts along dimension 0, may hold values from 0 to 15, each once within a row
- lengths: int32 [4], P('groups'), parts along dimension 0, may hold values from 1 to 128, as said below
Outputs:
- child_out: bfloat16 [32, 128, 4096], P(('groups', 'ctx')), parts along dimension 0
There are 2 independent parts, one for each index of `groups`. A program takes and returns all parts, laid end to end along the dimension named above; each array names one. Nothing has to cross between parts.
Inputs may be any that keep to these rules, and one draw needn't show every extreme that they name: `lengths`: some parent has all 128 positions valid.
All inputs are finite; a program needn't handle non-finite values.
Results may differ from a plain program's by a relative error of at most 0.0032.
Values may be sent and summed in bfloat16 or wider, within the bound.
No kernel may reach another device: no remote copies, remote signals or barrier semaphores. Data moves between devices by JAX's collectives and lax.ppermute only.
A program may use at most 64 MiB of HBM per device.

v0:
```python
import functools

import jax
import jax.numpy as jnp
from jax import lax
from jax.experimental import pallas as pl
from jax.experimental.pallas import tpu as pltpu
from jax.sharding import PartitionSpec as P

HD = 128
LOG2E = 1.4426950408889634
F32 = jnp.float32
BF16 = jnp.bfloat16
NEAR_HEADS, LAST_HEADS, OUT_HEADS, LOADS = 8, 8, 8, 4
VMEM = pl.BlockSpec(memory_space=pltpu.VMEM)
SMEM = pl.BlockSpec(memory_space=pltpu.SMEM)
HBM = pl.BlockSpec(memory_space=pltpu.HBM)


def in_hbm(*arrays):
    return [pltpu.with_memory_space_constraint(x, pltpu.HBM) for x in arrays]


def limit(mib):
    return pltpu.CompilerParams(vmem_limit_bytes=mib << 20)


def shard_rows(prompt_ref, parent_ref):
    prompt = prompt_ref[...].astype(F32)
    rows = []
    for p in range(parent_ref.shape[1]):
        piece = parent_ref[:, p].astype(F32)
        rows += [piece[:, 0, :], piece[:, 1, :]]
    return rows, [prompt[:, 0, :], prompt[:, 1, :]]


def shard_kernel(prompt_hbm, parent_hbm, out_ref, wide_ref, prompt_ref, parent_ref, sems):
    copies = [
        pltpu.make_async_copy(parent_hbm, parent_ref, sems.at[0]),
        pltpu.make_async_copy(prompt_hbm, prompt_ref, sems.at[1]),
    ]
    for copy in copies:
        copy.start()
    for copy in copies:
        copy.wait()
    pieces, shared = shard_rows(prompt_ref, parent_ref)
    rows = jnp.concatenate(pieces + shared, axis=0)
    out_ref[...] = rows.astype(BF16)
    wide_ref[...] = jnp.concatenate([rows, jnp.zeros_like(rows)], axis=0).astype(BF16)


def pack_kernel(fork_ref, prompt_ref, parent_ref, send_ref, table_ref):
    pieces, shared = shard_rows(prompt_ref, parent_ref)
    for p in range(parent_ref.shape[1]):
        table_ref[p] = jnp.concatenate(pieces[2 * p : 2 * p + 2] + shared, axis=0).astype(BF16)

    def place(d, carry):
        send_ref[d] = table_ref[fork_ref[d]]
        return carry

    lax.fori_loop(0, send_ref.shape[0], place, 0, unroll=min(8, send_ref.shape[0]))


def valid_keys(key, seg_rows, prompt_rows, counts, offsets, fork_ref, owner_ref, lengths_ref):
    n = owner_ref.shape[1]
    device = lax.axis_index("ctx")
    parent = fork_ref[device]
    place, row = jnp.full_like(key, -1), jnp.zeros_like(key)
    prompt = key < 0
    start, shard = 0, 0
    for count in counts:
        slot = key - start
        here = (slot >= 0) & (slot < count * seg_rows)
        place = jnp.where(here, shard + slot // seg_rows, place)
        row = jnp.where(here, slot % seg_rows, row)
        slot = slot - count * seg_rows
        here = (slot >= 0) & (slot < count * 2 * prompt_rows)
        prompt = prompt | (here & (slot % (2 * prompt_rows) < prompt_rows))
        start += count * (seg_rows + 2 * prompt_rows)
        shard += count
    block = place
    if offsets is not None:
        block = jnp.full_like(key, -1)
        for k in range(n):
            owner = device ^ jnp.where(device % 2 == 0, offsets[0][k], offsets[1][k])
            block = jnp.where(place == k, owner, block)

    def step(j, position):
        return jnp.where(block == owner_ref[parent, j], j * seg_rows + row, position)

    beyond = jnp.full_like(key, n * seg_rows)
    position = lax.fori_loop(0, n, step, beyond, unroll=min(16, n))
    return prompt | (position < lengths_ref[parent])


def split_keys(keys):
    keys = keys * (LOG2E * HD**-0.5)
    high = keys.astype(BF16)
    return jnp.concatenate([high, (keys - high.astype(F32)).astype(BF16)], axis=1)


def shard_keys(shards, seg_rows, prompt_rows, choice_ref, mask, fill, g):
    def rows(start, size):
        parts = [r[:, pl.ds(start, size), g * HD : (g + 1) * HD].astype(F32).reshape(-1, HD) for r in shards]
        return jnp.concatenate(parts, axis=0)

    def parent_rows(start):
        found = rows(start, seg_rows)
        for p in range(1, choice_ref.shape[0]):
            chosen = choice_ref[p, 0:1, :] > 0
            found = jnp.where(chosen, rows(start + p * 2 * seg_rows, seg_rows), found)
        return found

    prompt = rows(shards[0].shape[1] - 2 * prompt_rows, 2 * prompt_rows)
    keys = jnp.concatenate([parent_rows(0), prompt], axis=0)
    shifted = pltpu.roll(prompt, prompt.shape[0] - prompt_rows, 0)
    values = jnp.concatenate([parent_rows(seg_rows), shifted], axis=0)
    keys = split_keys(jnp.where(mask > 0, keys, fill))
    return keys, jnp.where(mask > 0, values, 0.0).astype(BF16)


def attend(q_ref, ready, causal, take, group, many):
    span, columns = q_ref.shape[1:]
    kept = {}

    def score(c):
        g = c * many // group
        if g not in kept:
            kept.clear()
            kept[g] = ready(g)
        keys, values = kept[g]
        query = jnp.concatenate([q_ref[0, :, i * HD : (i + 1) * HD] for i in range(c * many, (c + 1) * many)], axis=0)
        query = jnp.concatenate([query, query], axis=1)
        scores = lax.dot_general(keys, query, (((1,), (1,)), ((), ())), preferred_element_type=F32)
        if causal is not None:
            own = scores[:span] + causal
            scores = jnp.concatenate([own, scores[span:]], axis=0) if scores.shape[0] > span else own
        return scores, jnp.max(scores, axis=0, keepdims=True), values

    chunks = columns // HD // many
    made = score(0)
    for c in range(chunks):
        (scores, highest, values), made = made, score(c + 1) if c + 1 < chunks else None

        def weigh(top, scores=scores, values=values):
            weights = jnp.exp2(scores - top).astype(BF16)
            return jnp.dot(values, weights, preferred_element_type=F32)

        take(c, pl.ds(c * many * span, many * span), highest, weigh)


def load_kernel(sizes, *refs):
    ins, refs = refs[:5], refs[5:]
    q_ref, own_ref, choice_ref, *marks, raw_ref, fork_ref, owner_ref, lengths_ref, sems = refs
    tables = fork_ref, owner_ref, lengths_ref
    pairs = list(zip(ins, (*tables, raw_ref), strict=False))
    rows = q_ref.shape[1] // LOADS
    for k in range(LOADS):
        pairs.append((ins[4].at[:, pl.ds(k * rows, rows)], q_ref.at[:, pl.ds(k * rows, rows)]))
    copies = [pltpu.make_async_copy(src, dst, sems.at[k]) for k, (src, dst) in enumerate(pairs)]
    for copy in copies:
        copy.start()
    for copy in copies[:3]:
        copy.wait()
    parent = fork_ref[lax.axis_index("ctx")]
    for p in range(choice_ref.shape[0]):
        choice_ref[p] = jnp.full((8, HD), jnp.where(parent == p, 1.0, 0.0), F32)
    start = 0
    for across_ref, down_ref in zip(marks[::2], marks[1::2], strict=True):
        key = lax.broadcasted_iota(jnp.int32, (8, down_ref.shape[0]), 1)
        valid = valid_keys(key + start, *sizes, *tables).astype(F32)
        down_ref[...] = jnp.concatenate([valid] * (HD // 8), axis=0).T
        ahead = across_ref.shape[1] - down_ref.shape[0]
        if ahead:
            key = lax.broadcasted_iota(jnp.int32, (8, across_ref.shape[1]), 1) - ahead
            valid = ((key < 0) | valid_keys(key + start, *sizes, *tables)).astype(F32)
        across_ref[...] = jnp.concatenate([valid, valid], axis=0).astype(BF16)
        start += down_ref.shape[0]
    copies[3].wait()
    own_ref[...] = jnp.swapaxes(raw_ref[...], 0, 1)
    for copy in copies[4:]:
        copy.wait()


def near_kernel(seg_rows, prompt_rows, q_ref, own_ref, choice_ref, *refs):
    *others, state_ref, fill_ref = refs
    span = q_ref.shape[1]
    kv_heads = own_ref.shape[2] // HD
    group = q_ref.shape[2] // HD // kv_heads
    time = lax.broadcasted_iota(jnp.int32, (span, NEAR_HEADS * span), 1) % span
    causal = jnp.where(lax.broadcasted_iota(jnp.int32, time.shape, 0) <= time, 0.0, -jnp.inf)

    def ready(g):
        part = slice(g * HD, (g + 1) * HD)
        keys = own_ref[0, :, part].astype(F32)
        fill = keys[0:1]
        fill_ref[g] = jnp.broadcast_to(fill, (8, HD))
        keys, values = split_keys(keys), own_ref[1, :, part]
        if others:
            across_ref, down_ref, *shards = others
            more = shard_keys(shards, seg_rows, prompt_rows, choice_ref, down_ref[...], fill, g)
            keys, values = jnp.concatenate([keys, more[0]], axis=0), jnp.concatenate([values, more[1]], axis=0)
            ones = across_ref[...]
        else:
            ones = jnp.ones((16, span), BF16)
        return keys, jnp.concatenate([values.T, ones], axis=0)

    def take(c, lanes, highest, weigh):
        state_ref[: HD + 8, lanes] = weigh(highest)[: HD + 8]
        state_ref[HD + 8 :, lanes] = jnp.broadcast_to(highest, (8, highest.shape[1]))

    attend(q_ref, ready, causal, take, group, NEAR_HEADS)


def ready_kernel(seg_rows, prompt_rows, start, choice_ref, fill_ref, down_ref, *refs):
    *shards, keys_ref, values_ref = refs
    for g in range(fill_ref.shape[0]):
        mask = down_ref[start : start + keys_ref.shape[1]]
        made = shard_keys(shards, seg_rows, prompt_rows, choice_ref, mask, fill_ref[g, 0:1], g)
        keys_ref[g], values_ref[g] = made


def join_kernel(seg_rows, prompt_rows, count, q_ref, choice_ref, fill_ref, state_ref, across_ref, down_ref, *refs):
    shards, (*made_refs, out_ref, stage, sems) = refs[:count], refs[count:]
    many = LAST_HEADS
    span, columns = q_ref.shape[1:]
    group = columns // HD // fill_ref.shape[0]
    copies = []

    def ready(g):
        known = sum(r.shape[1] for r in made_refs[::2])
        keys, values = shard_keys(shards, seg_rows, prompt_rows, choice_ref, down_ref[known:], fill_ref[g, 0:1], g)
        if made_refs:
            keys = jnp.concatenate([*[r[g] for r in made_refs[::2]], keys], axis=0)
            values = jnp.concatenate([*[r[g] for r in made_refs[1::2]], values], axis=0)
        return keys, jnp.concatenate([values.T, across_ref[...]], axis=0)

    def take(c, lanes, highest, weigh):
        former = state_ref[HD + 8 :, lanes]
        top = jnp.maximum(former, highest)
        both = weigh(top[0:1])
        scale = jnp.exp2(former - top)
        total = state_ref[HD : HD + 8, lanes] * scale + both[HD : HD + 8]
        rows = (HD // 8, 8, -1)
        share = 1.0 / total
        scale = scale * share
        result = state_ref[:HD, lanes].reshape(rows) * scale[None] + both[:HD].reshape(rows) * share[None]
        result = result.reshape(HD, -1).astype(BF16)
        for k in range(many):
            i = c * many + k
            stage[:, i * HD : (i + 1) * HD] = result[:, k * span : (k + 1) * span].T
            if (i + 1) % OUT_HEADS == 0:
                part = pl.ds((i + 1 - OUT_HEADS) * HD, OUT_HEADS * HD)
                copies.append(pltpu.make_async_copy(stage.at[:, part], out_ref.at[0, :, part], sems.at[len(copies)]))
                copies[-1].start()

    attend(q_ref, ready, None, take, group, many)
    for copy in copies:
        copy.wait()


def permute(x, target, n):
    return lax.ppermute(x, "ctx", [(i, target(i)) for i in range(n)])


def pair_steps(n):
    return range(n // 4 - 2, 0, -1)


def gather_shards(shard, both, n):
    far, near = n - 4, 2
    mate = permute(shard, lambda i: i ^ 1, n)
    first = permute(shard, lambda i: i ^ far, n)
    both = lax.dynamic_update_slice(both, mate, (shard.shape[0], 0))
    pairs = pair_steps(n)
    wide = [permute(both, lambda i, j=j: i ^ (2 * (2 * j + i % 2)), n) for j in pairs]
    side = permute(shard, lambda i: i ^ near, n)
    passed = permute(first, lambda i: i ^ near, n)
    early = jnp.concatenate([first, side], axis=0)
    late = jnp.concatenate([*wide, passed], axis=0)
    early_theirs = permute(early, lambda i: i ^ 1, n)
    late_theirs = permute(late, lambda i: i ^ 1, n)
    straight, got = [far, near], []
    for core in range(2):
        steps = [2 * (2 * j + core) for j in pairs]
        got.append([*[o for d in steps for o in (d, d ^ 1)], far ^ near])
    close = [0, 1, *straight, *[o ^ 1 for o in straight]]
    offsets = [[*close, *got[core], *[o ^ 1 for o in got[1 - core]]] for core in range(2)]
    return [[shard, mate, early, early_theirs], [late], [late_theirs]], offsets


def use_gather(mesh_size, parents, seg_rows, prompt_rows):
    power = mesh_size >= 8 and mesh_size & (mesh_size - 1) == 0
    return power and parents * seg_rows + prompt_rows <= 2 * (seg_rows + prompt_rows)


def body(child_q, child_kv, prompt_kv, parent_kv, fork_list, owner_map, lengths):
    n = lax.axis_size("ctx")
    seg_rows, prompt_rows = parent_kv.shape[0], prompt_kv.shape[0]
    parents = parent_kv.shape[1]
    span, width = child_kv.shape[1], child_kv.shape[3]
    kv_heads = width // HD
    gather = use_gather(n, parents, seg_rows, prompt_rows)
    if gather:
        rows = 2 * (parents * seg_rows + prompt_rows)
        shard, both = pl.pallas_call(
            shard_kernel,
            out_shape=[jax.ShapeDtypeStruct((k * rows, width), BF16) for k in (1, 2)],
            in_specs=[HBM, HBM],
            out_specs=[VMEM, VMEM],
            scratch_shapes=[
                pltpu.VMEM(prompt_kv.shape, BF16),
                pltpu.VMEM(parent_kv.shape, BF16),
                pltpu.SemaphoreType.DMA((2,)),
            ],
            compiler_params=limit(2),
            name="shard",
        )(*in_hbm(prompt_kv, parent_kv))
        batches, offsets = gather_shards(shard, both, n)
    else:
        rows = 2 * (seg_rows + prompt_rows)
        send = pl.pallas_call(
            pack_kernel,
            out_shape=jax.ShapeDtypeStruct((n, rows, width), BF16),
            in_specs=[SMEM, VMEM, VMEM],
            out_specs=VMEM,
            scratch_shapes=[pltpu.VMEM((parents, rows, width), BF16)],
            name="pack",
        )(fork_list, prompt_kv, parent_kv)
        batches, offsets = [[], [lax.all_to_all(send, "ctx", split_axis=0, concat_axis=0, tiled=True)]], None
    batches = [[s.reshape(-1, rows, width) for s in batch] for batch in batches]
    sizes = [sum(s.shape[0] for s in batch) for batch in batches]
    counts = [sizes[0], sum(sizes[1:])]
    slots = seg_rows + 2 * prompt_rows
    heads = child_q.shape[2] // HD
    masks = []
    for k, count in enumerate(counts):
        if count:
            ahead = 0 if k else span
            masks += [((16, ahead + count * slots), BF16), ((count * slots, HD), F32)]
    query, own, choice, *marks = pl.pallas_call(
        functools.partial(load_kernel, (seg_rows, prompt_rows, sizes, offsets)),
        out_shape=[
            jax.ShapeDtypeStruct(child_q.shape, BF16),
            jax.ShapeDtypeStruct((2, span, width), BF16),
            jax.ShapeDtypeStruct((parents if gather else 1, 8, HD), F32),
            *[jax.ShapeDtypeStruct(*mask) for mask in masks],
        ],
        in_specs=[HBM] * 5,
        out_specs=[VMEM] * (3 + len(masks)),
        scratch_shapes=[
            pltpu.VMEM(child_kv.shape[1:], BF16),
            *[pltpu.SMEM(x.shape, jnp.int32) for x in (fork_list, owner_map, lengths)],
            pltpu.SemaphoreType.DMA((4 + LOADS,)),
        ],
        compiler_params=limit(8),
        name="load",
    )(*in_hbm(fork_list, owner_map, lengths, child_kv[0], child_q))
    marks = [marks[2 * k : 2 * k + 2] for k in range(len(marks) // 2)]
    marks = [[]] * (len(counts) - len(marks)) + marks
    state_shape = jax.ShapeDtypeStruct((HD + 16, heads * span), F32)
    state, fill = pl.pallas_call(
        functools.partial(near_kernel, seg_rows, prompt_rows),
        out_shape=[state_shape, jax.ShapeDtypeStruct((kv_heads, 8, HD), F32)],
        in_specs=[VMEM] * (3 + len(marks[0]) + len(batches[0])),
        out_specs=[VMEM] * 2,
        compiler_params=limit(16),
        name="near",
    )(query, own, choice, *marks[0], *batches[0])
    made = []
    for k in range(1, len(batches) - 1):
        made += pl.pallas_call(
            functools.partial(ready_kernel, seg_rows, prompt_rows, sum(sizes[1:k]) * slots),
            out_shape=[jax.ShapeDtypeStruct((kv_heads, sizes[k] * slots, m * HD), BF16) for m in (2, 1)],
            in_specs=[VMEM] * (3 + len(batches[k])),
            out_specs=[VMEM] * 2,
            compiler_params=limit(4),
        )(choice, fill, marks[1][1], *batches[k])
    last = batches[-1]
    return pl.pallas_call(
        functools.partial(join_kernel, seg_rows, prompt_rows, len(last)),
        out_shape=jax.ShapeDtypeStruct(child_q.shape, BF16),
        in_specs=[VMEM] * (6 + len(last) + len(made)),
        out_specs=HBM,
        scratch_shapes=[pltpu.VMEM(child_q.shape[1:], BF16), pltpu.SemaphoreType.DMA((heads // OUT_HEADS,))],
        compiler_params=limit(16 if gather else 48),
        name="join",
    )(query, choice, fill, state, *marks[1], *last, *made)


def solution(mesh):
    placed = (
        P(("groups", "ctx"), None, None),
        P(("groups", "ctx"), None, None, None),
        P(("groups", "ctx"), None, None),
        P(("groups", "ctx"), None, None, None),
        P("groups"),
        P("groups", None),
        P("groups"),
    )
    return jax.shard_map(
        body,
        mesh=mesh,
        in_specs=placed,
        out_specs=P(("groups", "ctx"), None, None),
        check_vma=False,
    )
```

profile of v0, /device:TPU:0, one launch (start us, length us, event | category | flops | bytes accessed | tf_op | source)
XLA Modules:
  0.0 22.1 jit_solution(9840653294380377041)
XLA Ops:
  0.0 0.8 %shard.1 = (bf16[40,512]{1,0:T(8,128)(2,1)S(1)}, bf16[80,512]{1,0:T(8,128)(2,1)S(1)}) custom-call(bf16[4,2,512]{2,1,0:T(2,128)(2,1)} %prompt_hbm.1, bf16[8,2,2,512]{3,2,1,0:T(2,128)(2,1)} %parent_hbm.1), custom_call_target="tpu_custom_call" | custom-call | tf_op jit(solution)/shard_map/shard/pallas_call | solution.py:306
  0.8 0.6 %collective-permute-start = (bf16[40,512]{1,0:T(8,128)(2,1)S(1)}, bf16[40,512]{1,0:T(8,128)(2,1)S(1)}, u32[]{:S(2)}, u32[]{:S(2)}) collective-permute-start(bf16[40,512]{1,0:T(8,128)(2,1)S(1)} %get-tuple-element.23), channel_id=1, source_target_pairs={{0,1},{1,0},{2,3},{3,2},{4,5},{5,4},{6,7},{7,6},{8,9},{9,8},{10,11... | collective-permute-start | bytes 122888 | tf_op jit(solution)/shard_map/ppermute | solution.py:263
  1.4 0.9 %collective-permute-done = bf16[40,512]{1,0:T(8,128)(2,1)S(1)} collective-permute-done((bf16[40,512]{1,0:T(8,128)(2,1)S(1)}, bf16[40,512]{1,0:T(8,128)(2,1)S(1)}, u32[]{:S(2)}, u32[]{:S(2)}) %collective-permute-start) | collective-permute-done | bytes 40992 | tf_op jit(solution)/shard_map/ppermute | solution.py:263
  2.2 3.9 %collective-permute-start.4 = (bf16[80,512]{1,0:T(8,128)(2,1)S(1)}, bf16[80,512]{1,0:T(8,128)(2,1)S(1)}, u32[]{:S(2)}, u32[]{:S(2)}) collective-permute-start(bf16[80,512]{1,0:T(8,128)(2,1)S(1)} %constant_dynamic-update-slice_fusion.5), channel_id=1, source_target_pairs={{0,8},{1,11},{2,10},{3,9},{4,12},{5,15},{6,14},{7,13},{8,0},{9,3},... | collective-permute-start | bytes 245768 | tf_op jit(solution)/shard_map/ppermute | solution.py:263
  6.2 1.3 %collective-permute-start.1 = (bf16[40,512]{1,0:T(8,128)(2,1)S(1)}, bf16[40,512]{1,0:T(8,128)(2,1)S(1)}, u32[]{:S(2)}, u32[]{:S(2)}) collective-permute-start(bf16[40,512]{1,0:T(8,128)(2,1)S(1)} %get-tuple-element.23), channel_id=1, source_target_pairs={{0,12},{1,13},{2,14},{3,15},{4,8},{5,9},{6,10},{7,11},{8,4},{9,5},... | collective-permute-start | bytes 122888 | tf_op jit(solution)/shard_map/ppermute | solution.py:263
  7.5 1.5 %collective-permute-start.2 = (bf16[40,512]{1,0:T(8,128)(2,1)S(1)}, bf16[40,512]{1,0:T(8,128)(2,1)S(1)}, u32[]{:S(2)}, u32[]{:S(2)}) collective-permute-start(bf16[40,512]{1,0:T(8,128)(2,1)S(1)} %get-tuple-element.23), channel_id=1, source_target_pairs={{0,2},{1,3},{2,0},{3,1},{4,6},{5,7},{6,4},{7,5},{8,10},{9,11},{10,... | collective-permute-start | bytes 122888 | tf_op jit(solution)/shard_map/ppermute | solution.py:263
  9.0 0.2 %collective-permute-start.5 = (bf16[80,512]{1,0:T(8,128)(2,1)S(1)}, bf16[80,512]{1,0:T(8,128)(2,1)S(1)}, u32[]{:S(2)}, u32[]{:S(2)}) collective-permute-start(bf16[80,512]{1,0:T(8,128)(2,1)S(1)} %constant_dynamic-update-slice_fusion.5), channel_id=1, source_target_pairs={{0,4},{1,7},{2,6},{3,5},{4,0},{5,3},{6,2},{7,1},{8,12},{9,15},{10,... | collective-permute-start | bytes 245768 | tf_op jit(solution)/shard_map/ppermute | solution.py:263
  9.2 3.2 %collective-permute-done.1 = bf16[40,512]{1,0:T(8,128)(2,1)S(1)} collective-permute-done((bf16[40,512]{1,0:T(8,128)(2,1)S(1)}, bf16[40,512]{1,0:T(8,128)(2,1)S(1)}, u32[]{:S(2)}, u32[]{:S(2)}) %collective-permute-start.1) | collective-permute-done | bytes 40992 | tf_op jit(solution)/shard_map/ppermute | solution.py:263
  12.4 1.2 %collective-permute-start.6 = (bf16[40,512]{1,0:T(8,128)(2,1)S(1)}, bf16[40,512]{1,0:T(8,128)(2,1)S(1)}, u32[]{:S(2)}, u32[]{:S(2)}) collective-permute-start(bf16[40,512]{1,0:T(8,128)(2,1)S(1)} %collective-permute-done.1), channel_id=1, source_target_pairs={{0,2},{1,3},{2,0},{3,1},{4,6},{5,7},{6,4},{7,5},{8,10},{9,11},{10,... | collective-permute-start | bytes 122888 | tf_op jit(solution)/shard_map/ppermute | solution.py:263
  13.6 0.0 collective-permute-done.4
  13.6 0.5 %collective-permute-done.5 = bf16[80,512]{1,0:T(8,128)(2,1)S(1)} collective-permute-done((bf16[80,512]{1,0:T(8,128)(2,1)S(1)}, bf16[80,512]{1,0:T(8,128)(2,1)S(1)}, u32[]{:S(2)}, u32[]{:S(2)}) %collective-permute-start.5) | collective-permute-done | bytes 81952 | tf_op jit(solution)/shard_map/ppermute | solution.py:263
  14.1 2.3 %collective-permute-done.6 = bf16[40,512]{1,0:T(8,128)(2,1)S(1)} collective-permute-done((bf16[40,512]{1,0:T(8,128)(2,1)S(1)}, bf16[40,512]{1,0:T(8,128)(2,1)S(1)}, u32[]{:S(2)}, u32[]{:S(2)}) %collective-permute-start.6) | collective-permute-done | bytes 40992 | tf_op jit(solution)/shard_map/ppermute | solution.py:263
  16.4 0.0 collective-permute-start.7
  16.4 0.0 collective-permute-done.2
  16.4 0.6 %collective-permute-start.3 = (bf16[80,512]{1,0:T(8,128)(2,1)S(1)}, bf16[80,512]{1,0:T(8,128)(2,1)S(1)}, u32[]{:S(2)}, u32[]{:S(2)}) collective-permute-start(bf16[80,512]{1,0:T(8,128)(2,1)S(1)} %constant_dynamic-update-slice_fusion), channel_id=1, source_target_pairs={{0,1},{1,0},{2,3},{3,2},{4,5},{5,4},{6,7},{7,6},{8,9},{9,8},{10,11... | collective-permute-start | bytes 245768 | tf_op jit(solution)/shard_map/ppermute | solution.py:263
  17.0 1.3 %load.1 = (bf16[1,128,4096]{2,1,0:T(8,128)(2,1)S(1)}, bf16[2,128,512]{2,1,0:T(8,128)(2,1)S(1)}, f32[2,8,128]{2,1,0:T(8,128)S(1)}, bf16[16,224]{1,0:T(8,128)(2,1)...) custom-call(s32[16]{0:T(128)} %refs_0_.1, s32[2,16]{1,0:T(2,128)} %refs_1_.1, ...), custom_call_target="tpu_custom_call" | custom-call | tf_op jit(solution)/shard_map/load/pallas_call | solution.py:341
  18.3 0.0 collective-permute-done.3
  18.4 1.4 %near.1 = (f32[144,4096]{1,0:T(8,128)S(1)}, f32[4,8,128]{2,1,0:T(8,128)S(1)}) custom-call(bf16[1,128,4096]{2,1,0:T(8,128)(2,1)S(1)} %get-tuple-element.18.q_ref, bf16[2,128,512]{2,1,0:T(8,128)(2,1)S(1)} %get-tuple-element.20.own_ref, f32[2,8,128]{2,1,0:T(8,128)S(1)} %get-tuple-element.19.choice_ref, bf16[16,224]{1,0:T(8,128)(2,1)S(1)} %get-tuple-element.21.refs_0_, ...), custom_call_target="tpu_custom_call" | custom-call | tf_op jit(solution)/shard_map/near/pallas_call | solution.py:362
  19.8 0.1 shard_map.73
  19.9 0.0 collective-permute-done.7
  19.9 2.2 %join.1 = bf16[1,128,4096]{2,1,0:T(8,128)(2,1)} custom-call(bf16[1,128,4096]{2,1,0:T(8,128)(2,1)S(1)} %get-tuple-element.18.q_ref, f32[2,8,128]{2,1,0:T(8,128)S(1)} %get-tuple-element.19.choice_ref, f32[4,8,128]{2,1,0:T(8,128)S(1)} %get-tuple-element.24.fill_ref, f32[144,4096]{1,0:T(8,128)S(1)} %get-tuple-element.25.state_ref, ...), custom_call_target="tpu_custom_call" | custom-call | tf_op jit(solution)/shard_map/join/pallas_call | solution.py:380
  (6 shorter events, 0.0 us)
Async XLA Ops:
  0.8 1.4 %collective-permute-start = (bf16[40,512]{1,0:T(8,128)(2,1)S(1)}, bf16[40,512]{1,0:T(8,128)(2,1)S(1)}, u32[]{:S(2)}, u32[]{:S(2)}) collective-permute-start(bf16[40,512]{1,0:T(8,128)(2,1)S(1)} %get-tuple-element.23), channel_id=1, source_target_pairs={{0,1},{1,0},{2,3},{3,2},{4,5},{5,4},{6,7},{7,6},{8,9},{9,8},{10,11... | collective-permute-start | bytes 122888 | tf_op jit(solution)/shard_map/ppermute | solution.py:263
  2.2 11.4 %collective-permute-start.4 = (bf16[80,512]{1,0:T(8,128)(2,1)S(1)}, bf16[80,512]{1,0:T(8,128)(2,1)S(1)}, u32[]{:S(2)}, u32[]{:S(2)}) collective-permute-start(bf16[80,512]{1,0:T(8,128)(2,1)S(1)} %constant_dynamic-update-slice_fusion.5), channel_id=1, source_target_pairs={{0,8},{1,11},{2,10},{3,9},{4,12},{5,15},{6,14},{7,13},{8,0},{9,3},... | collective-permute-start | bytes 245768 | tf_op jit(solution)/shard_map/ppermute | solution.py:263
  6.2 6.2 %collective-permute-start.1 = (bf16[40,512]{1,0:T(8,128)(2,1)S(1)}, bf16[40,512]{1,0:T(8,128)(2,1)S(1)}, u32[]{:S(2)}, u32[]{:S(2)}) collective-permute-start(bf16[40,512]{1,0:T(8,128)(2,1)S(1)} %get-tuple-element.23), channel_id=1, source_target_pairs={{0,12},{1,13},{2,14},{3,15},{4,8},{5,9},{6,10},{7,11},{8,4},{9,5},... | collective-permute-start | bytes 122888 | tf_op jit(solution)/shard_map/ppermute | solution.py:263
  7.5 8.9 %collective-permute-start.2 = (bf16[40,512]{1,0:T(8,128)(2,1)S(1)}, bf16[40,512]{1,0:T(8,128)(2,1)S(1)}, u32[]{:S(2)}, u32[]{:S(2)}) collective-permute-start(bf16[40,512]{1,0:T(8,128)(2,1)S(1)} %get-tuple-element.23), channel_id=1, source_target_pairs={{0,2},{1,3},{2,0},{3,1},{4,6},{5,7},{6,4},{7,5},{8,10},{9,11},{10,... | collective-permute-start | bytes 122888 | tf_op jit(solution)/shard_map/ppermute | solution.py:263
  9.0 5.1 %collective-permute-start.5 = (bf16[80,512]{1,0:T(8,128)(2,1)S(1)}, bf16[80,512]{1,0:T(8,128)(2,1)S(1)}, u32[]{:S(2)}, u32[]{:S(2)}) collective-permute-start(bf16[80,512]{1,0:T(8,128)(2,1)S(1)} %constant_dynamic-update-slice_fusion.5), channel_id=1, source_target_pairs={{0,4},{1,7},{2,6},{3,5},{4,0},{5,3},{6,2},{7,1},{8,12},{9,15},{10,... | collective-permute-start | bytes 245768 | tf_op jit(solution)/shard_map/ppermute | solution.py:263
  12.4 4.0 %collective-permute-start.6 = (bf16[40,512]{1,0:T(8,128)(2,1)S(1)}, bf16[40,512]{1,0:T(8,128)(2,1)S(1)}, u32[]{:S(2)}, u32[]{:S(2)}) collective-permute-start(bf16[40,512]{1,0:T(8,128)(2,1)S(1)} %collective-permute-done.1), channel_id=1, source_target_pairs={{0,2},{1,3},{2,0},{3,1},{4,6},{5,7},{6,4},{7,5},{8,10},{9,11},{10,... | collective-permute-start | bytes 122888 | tf_op jit(solution)/shard_map/ppermute | solution.py:263
  16.4 3.5 %collective-permute-start.7 = (bf16[200,512]{1,0:T(8,128)(2,1)S(1)}, bf16[200,512]{1,0:T(8,128)(2,1)S(1)}, u32[]{:S(2)}, u32[]{:S(2)}) collective-permute-start(bf16[200,512]{1,0:T(8,128)(2,1)S(1)} %constant_dynamic-update-slice_fusion.2), channel_id=1, source_target_pairs={{0,1},{1,0},{2,3},{3,2},{4,5},{5,4},{6,7},{7,6},{8,9},{9,8},{10,11... | collective-permute-start | bytes 614408 | tf_op jit(solution)/shard_map/ppermute | solution.py:263
  16.4 1.9 %collective-permute-start.3 = (bf16[80,512]{1,0:T(8,128)(2,1)S(1)}, bf16[80,512]{1,0:T(8,128)(2,1)S(1)}, u32[]{:S(2)}, u32[]{:S(2)}) collective-permute-start(bf16[80,512]{1,0:T(8,128)(2,1)S(1)} %constant_dynamic-update-slice_fusion), channel_id=1, source_target_pairs={{0,1},{1,0},{2,3},{3,2},{4,5},{5,4},{6,7},{7,6},{8,9},{9,8},{10,11... | collective-permute-start | bytes 245768 | tf_op jit(solution)/shard_map/ppermute | solution.py:263
where the time goes:
time: 22.3 us; the launch traced here: 22.1 us
  starting transfers between devices  9.3 us (42%)
  waiting for transfers between devices  6.83 us (31%)
  Pallas kernels  5.87 us (26%)
    ppermute x8, starting transfers between devices, permute(): return lax.ppermute(x, 'ctx', [(i, target(i)) for i in range(n)])  9.3 us
    ppermute x8, waiting for transfers between devices, permute(): return lax.ppermute(x, 'ctx', [(i, target(i)) for i in range(n)])  6.83 us
    pallas_call x1, Pallas kernels, body(): pl.pallas_call(functools.partial(join_kernel, seg_rows, prompt_rows, len(...  2.22 us
    pallas_call x1, Pallas kernels, body(): pl.pallas_call(functools.partial(near_kernel, seg_rows, prompt_rows), out...  1.44 us
    pallas_call x1, Pallas kernels, body(): pl.pallas_call(functools.partial(load_kernel, (seg_rows, prompt_rows, siz...  1.34 us
    pallas_call x1, Pallas kernels, body(): pl.pallas_call(shard_kernel, out_shape=[jax.ShapeDtypeStruct((k * rows, w...  0.81 us
  transfers between devices with their start and end apart: 8, of which 4 were waited for; matrix products, arithmetic and copies ran while one was open for 0% of the time, Pallas kernels for 13%

commit v1 on v0

--- a/solution.py
+++ b/solution.py
@@ -11,7 +11,7 @@
 LOG2E = 1.4426950408889634
 F32 = jnp.float32
 BF16 = jnp.bfloat16
-NEAR_HEADS, LAST_HEADS, OUT_HEADS, LOADS = 8, 8, 8, 4
+NEAR_HEADS, LAST_HEADS, OUT_HEADS, LOADS = 8, 8, 8, 1
 VMEM = pl.BlockSpec(memory_space=pltpu.VMEM)
 SMEM = pl.BlockSpec(memory_space=pltpu.SMEM)
 HBM = pl.BlockSpec(memory_space=pltpu.HBM)
@@ -277,16 +277,21 @@
     side = permute(shard, lambda i: i ^ near, n)
     passed = permute(first, lambda i: i ^ near, n)
     early = jnp.concatenate([first, side], axis=0)
-    late = jnp.concatenate([*wide, passed], axis=0)
+    soon = jnp.concatenate(wide[1:], axis=0)
+    late = jnp.concatenate([*wide[:1], passed], axis=0)
     early_theirs = permute(early, lambda i: i ^ 1, n)
+    soon_theirs = permute(soon, lambda i: i ^ 1, n)
     late_theirs = permute(late, lambda i: i ^ 1, n)
     straight, got = [far, near], []
     for core in range(2):
-        steps = [2 * (2 * j + core) for j in pairs]
-        got.append([*[o for d in steps for o in (d, d ^ 1)], far ^ near])
-    close = [0, 1, *straight, *[o ^ 1 for o in straight]]
-    offsets = [[*close, *got[core], *[o ^ 1 for o in got[1 - core]]] for core in range(2)]
-    return [[shard, mate, early, early_theirs], [late], [late_theirs]], offsets
+        steps = [[2 * (2 * j + core), 2 * (2 * j + core) ^ 1] for j in pairs]
+        got.append(([o for step in steps[1:] for o in step], [*steps[0], far ^ near]))
+    offsets = []
+    for core in range(2):
+        close = [0, 1, *straight, *[o ^ 1 for o in straight]]
+        others = [[o ^ 1 for o in part] for part in got[1 - core]]
+        offsets.append([*close, *got[core][0], *others[0], *got[core][1], *others[1]])
+    return [[shard, mate, early, early_theirs], [soon], [soon_theirs, late], [late_theirs]], offsets
 
 
 def use_gather(mesh_size, parents, seg_rows, prompt_rows):

time: 22.3 us -> 21.1 us (0.946)
  waiting for transfers between devices: 6.83 us -> 5.84 us
  starting transfers between devices: 9.3 us -> 9.01 us
    ppermute x8 -> x9, waiting for transfers between devices: 6.83 us -> 5.84 us  [permute(): return lax.ppermute(x, 'ctx', [(i, target(i)) for i in range(n)])]
    ppermute x8 -> x9, starting transfers between devices: 9.3 us -> 9.01 us  [permute(): return lax.ppermute(x, 'ctx', [(i, target(i)) for i in range(n)])]
  transfers between devices with their start and end apart: 8 -> 9, of which waited for: 4 -> 3; matrix products, arithmetic and copies ran while one was open for 0% -> 0% of each run, Pallas kernels for 13% -> 14%
where the time goes in v1:
time: 21.1 us; the launch traced here: 20.9 us
  starting transfers between devices  9.01 us (43%)
  Pallas kernels  5.94 us (28%)
  waiting for transfers between devices  5.84 us (28%)
    ppermute x9, starting transfers between devices, permute(): return lax.ppermute(x, 'ctx', [(i, target(i)) for i in range(n)])  9.01 us
    ppermute x9, waiting for transfers between devices, permute(): return lax.ppermute(x, 'ctx', [(i, target(i)) for i in range(n)])  5.84 us
    pallas_call x1, Pallas kernels, body(): pl.pallas_call(functools.partial(join_kernel, seg_rows, prompt_rows, len(...  2.21 us
    pallas_call x1, Pallas kernels, body(): pl.pallas_call(functools.partial(near_kernel, seg_rows, prompt_rows), out...  1.46 us
    pallas_call x1, Pallas kernels, body(): pl.pallas_call(functools.partial(load_kernel, (seg_rows, prompt_rows, siz...  1.36 us
    pallas_call x1, Pallas kernels, body(): pl.pallas_call(shard_kernel, out_shape=[jax.ShapeDtypeStruct((k * rows, w...  0.81 us
  transfers between devices with their start and end apart: 9, of which 3 were waited for; matrix products, arithmetic and copies ran while one was open for 0% of the time, Pallas kernels for 14%

profile of v1, /device:TPU:0, one launch (start us, length us, event | category | flops | bytes accessed | tf_op | source)
XLA Modules:
  0.0 20.9 jit_solution(14708111335345309876)
XLA Ops:
  0.0 0.8 %shard.1 = (bf16[40,512]{1,0:T(8,128)(2,1)S(1)}, bf16[80,512]{1,0:T(8,128)(2,1)S(1)}) custom-call(bf16[4,2,512]{2,1,0:T(2,128)(2,1)} %prompt_hbm.1, bf16[8,2,2,512]{3,2,1,0:T(2,128)(2,1)} %parent_hbm.1), custom_call_target="tpu_custom_call" | custom-call | tf_op jit(solution)/shard_map/shard/pallas_call | solution.py:311
  0.8 0.6 %collective-permute-start = (bf16[40,512]{1,0:T(8,128)(2,1)S(1)}, bf16[40,512]{1,0:T(8,128)(2,1)S(1)}, u32[]{:S(2)}, u32[]{:S(2)}) collective-permute-start(bf16[40,512]{1,0:T(8,128)(2,1)S(1)} %get-tuple-element.25), channel_id=1, source_target_pairs={{0,1},{1,0},{2,3},{3,2},{4,5},{5,4},{6,7},{7,6},{8,9},{9,8},{10,11... | collective-permute-start | bytes 122888 | tf_op jit(solution)/shard_map/ppermute | solution.py:263
  1.4 2.6 %collective-permute-start.2 = (bf16[40,512]{1,0:T(8,128)(2,1)S(1)}, bf16[40,512]{1,0:T(8,128)(2,1)S(1)}, u32[]{:S(2)}, u32[]{:S(2)}) collective-permute-start(bf16[40,512]{1,0:T(8,128)(2,1)S(1)} %get-tuple-element.25), channel_id=1, source_target_pairs={{0,2},{1,3},{2,0},{3,1},{4,6},{5,7},{6,4},{7,5},{8,10},{9,11},{10,... | collective-permute-start | bytes 122888 | tf_op jit(solution)/shard_map/ppermute | solution.py:263
  3.9 3.6 %collective-permute-start.1 = (bf16[40,512]{1,0:T(8,128)(2,1)S(1)}, bf16[40,512]{1,0:T(8,128)(2,1)S(1)}, u32[]{:S(2)}, u32[]{:S(2)}) collective-permute-start(bf16[40,512]{1,0:T(8,128)(2,1)S(1)} %get-tuple-element.25), channel_id=1, source_target_pairs={{0,12},{1,13},{2,14},{3,15},{4,8},{5,9},{6,10},{7,11},{8,4},{9,5},... | collective-permute-start | bytes 122888 | tf_op jit(solution)/shard_map/ppermute | solution.py:263
  7.5 0.0 collective-permute-done
  7.5 0.0 collective-permute-start.7
  7.5 0.8 %collective-permute-start.4 = (bf16[80,512]{1,0:T(8,128)(2,1)S(1)}, bf16[80,512]{1,0:T(8,128)(2,1)S(1)}, u32[]{:S(2)}, u32[]{:S(2)}) collective-permute-start(bf16[80,512]{1,0:T(8,128)(2,1)S(1)} %constant_dynamic-update-slice_fusion.4), channel_id=1, source_target_pairs={{0,8},{1,11},{2,10},{3,9},{4,12},{5,15},{6,14},{7,13},{8,0},{9,3},... | collective-permute-start | bytes 245768 | tf_op jit(solution)/shard_map/ppermute | solution.py:263
  8.3 1.8 %collective-permute-done.1 = bf16[40,512]{1,0:T(8,128)(2,1)S(1)} collective-permute-done((bf16[40,512]{1,0:T(8,128)(2,1)S(1)}, bf16[40,512]{1,0:T(8,128)(2,1)S(1)}, u32[]{:S(2)}, u32[]{:S(2)}) %collective-permute-start.1) | collective-permute-done | bytes 40992 | tf_op jit(solution)/shard_map/ppermute | solution.py:263
  10.2 0.0 collective-permute-start.5
  10.2 2.8 %collective-permute-done.4 = bf16[80,512]{1,0:T(8,128)(2,1)S(1)} collective-permute-done((bf16[80,512]{1,0:T(8,128)(2,1)S(1)}, bf16[80,512]{1,0:T(8,128)(2,1)S(1)}, u32[]{:S(2)}, u32[]{:S(2)}) %collective-permute-start.4) | collective-permute-done | bytes 81952 | tf_op jit(solution)/shard_map/ppermute | solution.py:263
  13.0 1.2 %collective-permute-done.5 = bf16[40,512]{1,0:T(8,128)(2,1)S(1)} collective-permute-done((bf16[40,512]{1,0:T(8,128)(2,1)S(1)}, bf16[40,512]{1,0:T(8,128)(2,1)S(1)}, u32[]{:S(2)}, u32[]{:S(2)}) %collective-permute-start.5) | collective-permute-done | bytes 40992 | tf_op jit(solution)/shard_map/ppermute | solution.py:263
  14.2 1.0 %collective-permute-start.6 = (bf16[120,512]{1,0:T(8,128)(2,1)S(1)}, bf16[120,512]{1,0:T(8,128)(2,1)S(1)}, u32[]{:S(2)}, u32[]{:S(2)}) collective-permute-start(bf16[120,512]{1,0:T(8,128)(2,1)S(1)} %constant_dynamic-update-slice_fusion.2), channel_id=1, source_target_pairs={{0,1},{1,0},{2,3},{3,2},{4,5},{5,4},{6,7},{7,6},{8,9},{9,8},{10,11... | collective-permute-start | bytes 368648 | tf_op jit(solution)/shard_map/ppermute | solution.py:263
  15.2 0.0 collective-permute-done.2
  15.2 0.1 collective-permute-start.3
  15.3 0.0 collective-permute-done.7
  15.3 0.4 %collective-permute-start.8 = (bf16[80,512]{1,0:T(8,128)(2,1)S(1)}, bf16[80,512]{1,0:T(8,128)(2,1)S(1)}, u32[]{:S(2)}, u32[]{:S(2)}) collective-permute-start(bf16[80,512]{1,0:T(8,128)(2,1)S(1)} %collective-permute-done.7), channel_id=1, source_target_pairs={{0,1},{1,0},{2,3},{3,2},{4,5},{5,4},{6,7},{7,6},{8,9},{9,8},{10,11... | collective-permute-start | bytes 245768 | tf_op jit(solution)/shard_map/ppermute | solution.py:263
  15.7 1.4 %load.1 = (bf16[1,128,4096]{2,1,0:T(8,128)(2,1)S(1)}, bf16[2,128,512]{2,1,0:T(8,128)(2,1)S(1)}, f32[2,8,128]{2,1,0:T(8,128)S(1)}, bf16[16,224]{1,0:T(8,128)(2,1)...) custom-call(s32[16]{0:T(128)} %refs_0_.1, s32[2,16]{1,0:T(2,128)} %refs_1_.1, ...), custom_call_target="tpu_custom_call" | custom-call | tf_op jit(solution)/shard_map/load/pallas_call | solution.py:346
  17.1 0.0 collective-permute-done.3
  17.1 1.5 %near.1 = (f32[144,4096]{1,0:T(8,128)S(1)}, f32[4,8,128]{2,1,0:T(8,128)S(1)}) custom-call(bf16[1,128,4096]{2,1,0:T(8,128)(2,1)S(1)} %get-tuple-element.20.q_ref, bf16[2,128,512]{2,1,0:T(8,128)(2,1)S(1)} %get-tuple-element.22.own_ref, f32[2,8,128]{2,1,0:T(8,128)S(1)} %get-tuple-element.21.choice_ref, bf16[16,224]{1,0:T(8,128)(2,1)S(1)} %get-tuple-element.23.refs_0_, ...), custom_call_target="tpu_custom_call" | custom-call | tf_op jit(solution)/shard_map/near/pallas_call | solution.py:367
  18.6 0.0 collective-permute-done.8
  18.6 0.1 shard_map.74
  18.7 0.0 collective-permute-done.6
  18.7 2.2 %join.1 = bf16[1,128,4096]{2,1,0:T(8,128)(2,1)} custom-call(bf16[1,128,4096]{2,1,0:T(8,128)(2,1)S(1)} %get-tuple-element.20.q_ref, f32[2,8,128]{2,1,0:T(8,128)S(1)} %get-tuple-element.21.choice_ref, f32[4,8,128]{2,1,0:T(8,128)S(1)} %get-tuple-element.26.fill_ref, f32[144,4096]{1,0:T(8,128)S(1)} %get-tuple-element.27.state_ref, ...), custom_call_target="tpu_custom_call" | custom-call | tf_op jit(solution)/shard_map/join/pallas_call | solution.py:385
  (6 shorter events, 0.1 us)
Async XLA Ops:
  0.8 6.7 %collective-permute-start = (bf16[40,512]{1,0:T(8,128)(2,1)S(1)}, bf16[40,512]{1,0:T(8,128)(2,1)S(1)}, u32[]{:S(2)}, u32[]{:S(2)}) collective-permute-start(bf16[40,512]{1,0:T(8,128)(2,1)S(1)} %get-tuple-element.25), channel_id=1, source_target_pairs={{0,1},{1,0},{2,3},{3,2},{4,5},{5,4},{6,7},{7,6},{8,9},{9,8},{10,11... | collective-permute-start | bytes 122888 | tf_op jit(solution)/shard_map/ppermute | solution.py:263
  1.4 13.8 %collective-permute-start.2 = (bf16[40,512]{1,0:T(8,128)(2,1)S(1)}, bf16[40,512]{1,0:T(8,128)(2,1)S(1)}, u32[]{:S(2)}, u32[]{:S(2)}) collective-permute-start(bf16[40,512]{1,0:T(8,128)(2,1)S(1)} %get-tuple-element.25), channel_id=1, source_target_pairs={{0,2},{1,3},{2,0},{3,1},{4,6},{5,7},{6,4},{7,5},{8,10},{9,11},{10,... | collective-permute-start | bytes 122888 | tf_op jit(solution)/shard_map/ppermute | solution.py:263
  3.9 6.2 %collective-permute-start.1 = (bf16[40,512]{1,0:T(8,128)(2,1)S(1)}, bf16[40,512]{1,0:T(8,128)(2,1)S(1)}, u32[]{:S(2)}, u32[]{:S(2)}) collective-permute-start(bf16[40,512]{1,0:T(8,128)(2,1)S(1)} %get-tuple-element.25), channel_id=1, source_target_pairs={{0,12},{1,13},{2,14},{3,15},{4,8},{5,9},{6,10},{7,11},{8,4},{9,5},... | collective-permute-start | bytes 122888 | tf_op jit(solution)/shard_map/ppermute | solution.py:263
  7.5 7.7 %collective-permute-start.7 = (bf16[80,512]{1,0:T(8,128)(2,1)S(1)}, bf16[80,512]{1,0:T(8,128)(2,1)S(1)}, u32[]{:S(2)}, u32[]{:S(2)}) collective-permute-start(bf16[80,512]{1,0:T(8,128)(2,1)S(1)} %constant_dynamic-update-slice_fusion.4), channel_id=1, source_target_pairs={{0,4},{1,7},{2,6},{3,5},{4,0},{5,3},{6,2},{7,1},{8,12},{9,15},{10,... | collective-permute-start | bytes 245768 | tf_op jit(solution)/shard_map/ppermute | solution.py:263
  7.5 5.4 %collective-permute-start.4 = (bf16[80,512]{1,0:T(8,128)(2,1)S(1)}, bf16[80,512]{1,0:T(8,128)(2,1)S(1)}, u32[]{:S(2)}, u32[]{:S(2)}) collective-permute-start(bf16[80,512]{1,0:T(8,128)(2,1)S(1)} %constant_dynamic-update-slice_fusion.4), channel_id=1, source_target_pairs={{0,8},{1,11},{2,10},{3,9},{4,12},{5,15},{6,14},{7,13},{8,0},{9,3},... | collective-permute-start | bytes 245768 | tf_op jit(solution)/shard_map/ppermute | solution.py:263
  10.2 4.0 %collective-permute-start.5 = (bf16[40,512]{1,0:T(8,128)(2,1)S(1)}, bf16[40,512]{1,0:T(8,128)(2,1)S(1)}, u32[]{:S(2)}, u32[]{:S(2)}) collective-permute-start(bf16[40,512]{1,0:T(8,128)(2,1)S(1)} %collective-permute-done.1), channel_id=1, source_target_pairs={{0,2},{1,3},{2,0},{3,1},{4,6},{5,7},{6,4},{7,5},{8,10},{9,11},{10,... | collective-permute-start | bytes 122888 | tf_op jit(solution)/shard_map/ppermute | solution.py:263
  14.2 4.5 %collective-permute-start.6 = (bf16[120,512]{1,0:T(8,128)(2,1)S(1)}, bf16[120,512]{1,0:T(8,128)(2,1)S(1)}, u32[]{:S(2)}, u32[]{:S(2)}) collective-permute-start(bf16[120,512]{1,0:T(8,128)(2,1)S(1)} %constant_dynamic-update-slice_fusion.2), channel_id=1, source_target_pairs={{0,1},{1,0},{2,3},{3,2},{4,5},{5,4},{6,7},{7,6},{8,9},{9,8},{10,11... | collective-permute-start | bytes 368648 | tf_op jit(solution)/shard_map/ppermute | solution.py:263
  15.2 1.9 %collective-permute-start.3 = (bf16[80,512]{1,0:T(8,128)(2,1)S(1)}, bf16[80,512]{1,0:T(8,128)(2,1)S(1)}, u32[]{:S(2)}, u32[]{:S(2)}) collective-permute-start(bf16[80,512]{1,0:T(8,128)(2,1)S(1)} %constant_dynamic-update-slice_fusion), channel_id=1, source_target_pairs={{0,1},{1,0},{2,3},{3,2},{4,5},{5,4},{6,7},{7,6},{8,9},{9,8},{10,11... | collective-permute-start | bytes 245768 | tf_op jit(solution)/shard_map/ppermute | solution.py:263
  15.3 3.3 %collective-permute-start.8 = (bf16[80,512]{1,0:T(8,128)(2,1)S(1)}, bf16[80,512]{1,0:T(8,128)(2,1)S(1)}, u32[]{:S(2)}, u32[]{:S(2)}) collective-permute-start(bf16[80,512]{1,0:T(8,128)(2,1)S(1)} %collective-permute-done.7), channel_id=1, source_target_pairs={{0,1},{1,0},{2,3},{3,2},{4,5},{5,4},{6,7},{7,6},{8,9},{9,8},{10,11... | collective-permute-start | bytes 245768 | tf_op jit(solution)/shard_map/ppermute | solution.py:263
